TPU v7x, 32 devices: a whole 2x2x4 slice. The times are simulated.
32 devices in a mesh: qx: 8 (over z, y), qy: 4 (over x, core).
Axes of the slice: x: 2, y: 2, z: 4, core: 2. Of those that a mesh axis runs over, the one named last changes fastest.
Arguments:
- vectors: bfloat16 [64, 256, 512], P(None, 'qx', 'qy'), may hold values from -6 to 6
- near_tiles: bfloat16 [16, 32, 3, 256, 256], P('qx', 'qy'), may hold values from -0.21875 to 0.21875
- near_offset: int32 [16, 32, 3], P('qx', 'qy'), may hold values from 0 to 8, as said below
- col_basis: bfloat16 [16, 32, 64, 256], P('qx', 'qy'), may hold values from -0.375 to 0.375
- row_basis: bfloat16 [16, 32, 64, 256], P('qx', 'qy'), may hold values from -0.375 to 0.375
- up_transfer: float32 [16, 32, 64, 64], P('qx', 'qy'), may hold values from -0.375 to 0.375
- down_transfer: float32 [16, 32, 64, 64], P('qx', 'qy'), may hold values from -0.75 to 0.75
- coupling: float32 [32, 128, 64, 64], P(('qx', 'qy')), may hold values from -0.75 to 0.75
- couple_dest: int32 [32, 128], replicated, may hold values from -1 to 31, as said below
- couple_target: int32 [32, 128], replicated, may hold values from 0 to 19, as said below
Outputs:
- product: float32 [64, 256, 512], P(None, 'qx', 'qy')
Inputs may be any that keep to these rules, and one draw needn't show every extreme that they name: `couple_dest`: in each row (source device) no destination device appears more than 4 times; in every draw one destination device appears exactly 4 times in every row; -1 marks a padded slot. `couple_target`: slots below 96 name a leaf cluster (0 to 15), the others a parent cluster (16 to 19) of the target device. `near_offset`: the 3 codes of a leaf are distinct; code o reads the leaf at offset (o // 3 - 1, o % 3 - 1).
All inputs are finite; a program needn't handle non-finite values.
Results may differ from a plain program's by a relative error of at most 0.0003.
Values may be sent and summed in bfloat16 or wider, within the bound.
A program may use at most 64 MiB of HBM per device.

v0:
```python
import jax
import jax.numpy as jnp
from jax import lax
from jax.experimental import pallas as pl
from jax.experimental.pallas import tpu as pltpu
from jax.sharding import PartitionSpec as P

LS = 16
K0 = 6
K1 = 8


ANY = pl.BlockSpec(memory_space=pl.ANY)
VM = pl.BlockSpec(memory_space=pltpu.VMEM)
SM = pl.BlockSpec(memory_space=pltpu.SMEM)
TOP = 14


def halves(value):
    high = value.astype(jnp.bfloat16)
    return high, (value - high.astype(jnp.float32)).astype(jnp.bfloat16)


def product_of(left, right):
    lh, ll = halves(left)
    rh, rl = halves(right)
    return jnp.dot(
        jnp.concatenate([lh, ll, lh, ll], axis=1),
        jnp.concatenate([rh, rh, rl, rl], axis=0),
        preferred_element_type=jnp.float32,
    )


def contributions(leaf_count, upper_count, slot_ref, coup_ref, leaf_ref, upper_ref, out_ref, max_ref, mats_ref, held):
    rank = coup_ref.shape[1]
    half = rank // 2
    held[held.shape[0] - 1] = jnp.zeros_like(held[0])

    def group(first, count, coef):
        mats = mats_ref[pl.ds(first, count)].reshape(count * rank, rank)
        res = product_of(mats, coef)
        for q in range(count):
            one = res[q * rank : (q + 1) * rank]
            held[first + q] = jnp.concatenate([one[:half], one[half:]], axis=1)

    def leaf_step(m, carry):
        group(m * K0, K0, leaf_ref[m])
        return carry

    def upper_step(m, carry):
        group(leaf_count * K0 + m * K1, K1, upper_ref[m])
        return carry

    def place(p, carry):
        value = held[slot_ref[p]]
        out_ref[p] = value
        max_ref[pl.ds(p, 1), :] = jnp.max(jnp.abs(value), axis=0, keepdims=True)
        return carry

    def turn(r, carry):
        mats_ref[:, r, :] = coup_ref[r].T
        return carry

    lax.fori_loop(0, rank, turn, 0, unroll=4)
    lax.fori_loop(0, leaf_count, leaf_step, 0, unroll=4)
    lax.fori_loop(0, upper_count, upper_step, 0, unroll=2)
    lax.fori_loop(0, out_ref.shape[0], place, 0, unroll=4)


def first_kernel(
    leaf_count,
    upper_count,
    width_x,
    width_y,
    slot_ref,
    coup_ref,
    leaf_ref,
    upper_ref,
    vec_ref,
    edge_ref,
    out_ref,
    max_ref,
    rows_ref,
    cols_ref,
    mats_ref,
    held,
    send_sem,
    recv_sem,
):
    here_x = lax.axis_index("qx")
    here_y = lax.axis_index("qy")
    rows = vec_ref.shape[1]
    leaf_x = edge_ref.shape[1]
    steps = [(1, 0), (-1, 0), (0, 1), (0, -1), (1, 1), (1, -1), (-1, 1), (-1, -1)]

    def present(dx, dy):
        x = here_x + dx
        y = here_y + dy
        return (x >= 0) & (x < width_x) & (y >= 0) & (y < width_y)

    def copy_of(n):
        dx, dy = steps[n]
        if dy == 0:
            first = rows - LS if dx > 0 else 0
            src = vec_ref.at[:, pl.ds(first, LS), :]
            dst = rows_ref.at[0 if dx > 0 else 1]
        else:
            side = 1 if dy > 0 else 0
            if dx == 0:
                src = edge_ref.at[side]
                dst = cols_ref.at[1 - side, pl.ds(1, leaf_x)]
            else:
                src = edge_ref.at[side, leaf_x - 1 if dx > 0 else 0]
                dst = cols_ref.at[1 - side, 0 if dx > 0 else leaf_x + 1]
        return pltpu.make_async_remote_copy(
            src_ref=src,
            dst_ref=dst,
            send_sem=send_sem.at[n],
            recv_sem=recv_sem.at[n],
            device_id=(here_x + dx, here_y + dy),
            device_id_type=pl.DeviceIdType.MESH,
        )

    barrier = pltpu.get_barrier_semaphore()
    for dx, dy in steps:

        @pl.when(present(dx, dy))
        def _():
            pl.semaphore_signal(
                barrier,
                inc=1,
                device_id=(here_x + dx, here_y + dy),
                device_id_type=pl.DeviceIdType.MESH,
            )

    spans = []
    for here, width in ((here_x, width_x), (here_y, width_y)):
        spans.append(1 + (here > 0).astype(jnp.int32) + (here < width - 1).astype(jnp.int32))
    pl.semaphore_wait(barrier, spans[0] * spans[1] - 1)

    for n, (dx, dy) in enumerate(steps):

        @pl.when(present(dx, dy))
        def _():
            copy_of(n).start()

    contributions(
        leaf_count, upper_count, slot_ref, coup_ref, leaf_ref, upper_ref, out_ref, max_ref, mats_ref, held
    )

    for n, (dx, dy) in enumerate(steps):

        @pl.when(present(dx, dy))
        def _():
            copy_of(n).wait_send()

        @pl.when(present(-dx, -dy))
        def _():
            copy_of(n).wait_recv()


def near_kernel(leaf_y, off_ref, tiles_ref, grid_ref, out_ref):
    vecs = grid_ref.shape[2]
    per = tiles_ref.shape[0]
    for u in range(per):
        m = pl.program_id(0) * per + u
        i = m // leaf_y
        j = lax.rem(m, leaf_y)
        total = None
        for k in range(tiles_ref.shape[1]):
            o = off_ref[m, k]
            x = (i + o // 3) * LS
            y = pl.multiple_of((j + lax.rem(o, 3)) * LS, LS)
            block = grid_ref[pl.ds(x, LS), pl.ds(y, LS), :].reshape(LS * LS, vecs)
            term = jnp.dot(tiles_ref[u, k], block, preferred_element_type=jnp.float32)
            total = term if total is None else total + term
        out_ref[u] = total


def far_kernel(leaf_x, leaf_y, tgt_ref, recv_ref, down_ref, row_ref, near_ref, out_ref, acc, full):
    leaf_count = leaf_x * leaf_y
    half = acc.shape[2] // 2
    acc[...] = jnp.zeros_like(acc)

    def add(r, carry):
        t = tgt_ref[r]
        acc[t] = acc[t] + recv_ref[r]
        return carry

    lax.fori_loop(0, recv_ref.shape[0], add, 0, unroll=4)

    def unfolded(n):
        value = acc[n]
        return jnp.concatenate([value[:, :half], value[:, half:]], axis=0)

    def leaf(m, carry):
        j = lax.rem(m, leaf_y)
        coef = unfolded(m) + product_of(down_ref[m], unfolded(leaf_count + j // 2))
        high, low = halves(coef)
        basis = row_ref[m]
        far = lax.dot_general(
            jnp.concatenate([basis, basis], axis=0),
            jnp.concatenate([high, low], axis=0),
            (((0,), (0,)), ((), ())),
            preferred_element_type=jnp.float32,
        )
        full[m] = near_ref[m] + far
        return carry

    lax.fori_loop(0, leaf_count, leaf, 0, unroll=4)
    for a in range(leaf_x):
        for i in range(LS):
            rows = [full[a * leaf_y + h, i * LS : (i + 1) * LS, :] for h in range(leaf_y)]
            out_ref[:, a * LS + i, :] = jnp.concatenate(rows, axis=0).T


def body(
    vectors,
    near_tiles,
    near_offset,
    col_basis,
    row_basis,
    up_transfer,
    down_transfer,
    coupling,
    couple_dest,
    couple_target,
):
    precise = lax.Precision.HIGHEST
    f32 = jnp.float32
    shape = jax.ShapeDtypeStruct
    width_x = lax.axis_size("qx")
    width_y = lax.axis_size("qy")
    devices = width_x * width_y
    vec_count, rows_x, rows_y = vectors.shape
    leaf_x = rows_x // LS
    leaf_y = rows_y // LS
    leaf_count = leaf_x * leaf_y
    upper_count = leaf_y // 2
    cluster_count = leaf_count + upper_count
    rank_size = coupling.shape[2]
    slot_count = coupling.shape[1]
    capacity = (slot_count + devices - 1) // devices
    near_count = near_tiles.shape[2]
    points = LS * LS
    fold = (rank_size // 2, 2 * vec_count)
    my_index = lax.axis_index("qx") * width_y + lax.axis_index("qy")

    minor = vectors.transpose(1, 2, 0)
    strips = jnp.stack([minor[:, :LS], minor[:, rows_y - LS :]]).reshape(2, leaf_x, LS, LS, vec_count)
    strips = jnp.concatenate([strips[:, :, : LS // 2], strips[:, :, LS // 2 :]], axis=-1)

    blocks = (
        vectors.reshape(vec_count, leaf_x, LS, leaf_y, LS)
        .transpose(1, 3, 0, 2, 4)
        .reshape(leaf_x, leaf_y, vec_count, points)
    )
    leaf_coef = jnp.einsum("ijrp,ijvp->ijrv", col_basis, blocks, preferred_element_type=f32)
    lifted = jnp.einsum("ijrs,ijsv->ijrv", up_transfer, leaf_coef, precision=precise)
    upper_coef = lifted.reshape(leaf_x, upper_count, 2, rank_size, vec_count).sum(axis=(0, 2))

    own_dest = lax.dynamic_index_in_dim(couple_dest, my_index, 0, keepdims=False)
    slot_ident = jnp.arange(slot_count, dtype=jnp.int32)
    same_dest = own_dest[:, None] == own_dest[None, :]
    earlier = slot_ident[:, None] > slot_ident[None, :]
    order_in = jnp.sum((same_dest & earlier).astype(jnp.int32), axis=1)
    spare_row = devices * capacity
    position = jnp.where(own_dest >= 0, own_dest * capacity + order_in, spare_row)
    filled = position[None, :] == jnp.arange(spare_row, dtype=jnp.int32)[:, None]
    slot_of = slot_count + jnp.sum(jnp.where(filled, slot_ident - slot_count, 0), axis=1)
    kind = vectors.dtype
    placed, peaks, near_rows, near_cols = pl.pallas_call(
        lambda *refs: first_kernel(leaf_count, upper_count, width_x, width_y, *refs),
        out_shape=(
            shape((spare_row,) + fold, f32),
            shape((spare_row, fold[1]), f32),
            shape((2, vec_count, LS, rows_y), kind),
            shape((2, leaf_x + 2, LS // 2, LS, 2 * vec_count), kind),
        ),
        in_specs=[SM, VM, VM, VM, ANY, ANY],
        out_specs=(VM, VM, ANY, ANY),
        scratch_shapes=[
            pltpu.VMEM((slot_count, rank_size, rank_size), f32),
            pltpu.VMEM((slot_count + 1,) + fold, f32),
            pltpu.SemaphoreType.DMA((8,)),
            pltpu.SemaphoreType.DMA((8,)),
        ],
        compiler_params=pltpu.CompilerParams(collective_id=0, has_side_effects=True),
        name="contrib",
    )(
        slot_of,
        coupling[0].transpose(1, 2, 0),
        leaf_coef.reshape(leaf_count, rank_size, vec_count),
        upper_coef,
        vectors,
        strips,
    )

    peak = jnp.max(peaks, axis=1)
    power = jnp.ceil(jnp.log2(jnp.maximum(peak, 1e-30)))
    scaled = placed * jnp.exp2(TOP - power)[:, None, None]
    notes = jnp.broadcast_to(power.reshape(devices, capacity, 1), (devices, capacity, fold[1]))
    outgoing = jnp.concatenate(
        [
            scaled.reshape(devices, capacity * fold[0], fold[1]).astype(jnp.float16),
            notes.astype(jnp.float16),
        ],
        axis=1,
    )
    outgoing, near_rows, near_cols = lax.optimization_barrier((outgoing, near_rows, near_cols))
    arrived = lax.all_to_all(outgoing, ("qx", "qy"), split_axis=0, concat_axis=0, tiled=True)

    here_x = lax.axis_index("qx")
    here_y = lax.axis_index("qy")
    has_x = jnp.stack([here_x > 0, here_x < width_x - 1])
    has_y = jnp.stack([here_y > 0, here_y < width_y - 1])
    near_rows = jnp.where(has_x[:, None, None, None], near_rows, 0).transpose(0, 2, 3, 1)
    tall = jnp.concatenate([near_rows[0], minor, near_rows[1]], axis=0)
    along = jnp.concatenate([has_x[:1], jnp.ones((leaf_x,), bool), has_x[1:]])
    valid = has_y[:, None] & along[None, :]
    near_cols = jnp.where(valid[:, :, None, None, None], near_cols, 0)
    near_cols = jnp.concatenate(
        [near_cols[..., :vec_count], near_cols[..., vec_count:]], axis=2
    ).reshape(2, rows_x + 2 * LS, LS, vec_count)
    grid = jnp.concatenate([near_cols[0], tall, near_cols[1]], axis=1)
    per = 4 if leaf_count % 4 == 0 else 1
    near = pl.pallas_call(
        lambda *refs: near_kernel(leaf_y, *refs),
        grid=(leaf_count // per,),
        out_shape=shape((leaf_count, points, vec_count), f32),
        in_specs=[
            SM,
            pl.BlockSpec((per, near_count, points, points), lambda m: (m, 0, 0, 0)),
            VM,
        ],
        out_specs=pl.BlockSpec((per, points, vec_count), lambda m: (m, 0, 0)),
        cost_estimate=pl.CostEstimate(
            flops=2 * leaf_count * near_count * points * points * vec_count,
            bytes_accessed=leaf_count * near_count * points * points * 2,
            transcendentals=0,
        ),
        name="near",
    )(
        near_offset.reshape(leaf_count, near_count),
        near_tiles.reshape(leaf_count, near_count, points, points),
        grid,
    )

    matches = couple_dest == my_index
    counts = matches.astype(jnp.int32)
    order = jnp.cumsum(counts, axis=-1) - counts
    landing = matches[:, None, :] & (order[:, None, :] == jnp.arange(capacity, dtype=jnp.int32)[None, :, None])
    target = cluster_count + jnp.sum(
        jnp.where(landing, couple_target[:, None, :] - cluster_count, 0), axis=-1
    )

    rows = capacity * fold[0]
    exponent = arrived[:, rows:, :1].astype(f32).reshape(spare_row, 1, 1)
    recv = arrived[:, :rows].astype(f32).reshape((spare_row,) + fold) * jnp.exp2(exponent - TOP)
    return pl.pallas_call(
        lambda *refs: far_kernel(leaf_x, leaf_y, *refs),
        out_shape=shape((vec_count, rows_x, rows_y), f32),
        in_specs=[SM, VM, VM, VM, VM],
        out_specs=VM,
        scratch_shapes=[
            pltpu.VMEM((cluster_count + 1,) + fold, f32),
            pltpu.VMEM((leaf_count, points, vec_count), f32),
        ],
        name="far",
    )(
        target.reshape(spare_row),
        recv,
        down_transfer.reshape(leaf_count, rank_size, rank_size),
        row_basis.reshape(leaf_count, rank_size, points),
        near,
    )


def solution(mesh):
    return jax.shard_map(
        body,
        mesh=mesh,
        in_specs=(
            P(None, "qx", "qy"),
            P("qx", "qy", None, None, None),
            P("qx", "qy", None),
            P("qx", "qy", None, None),
            P("qx", "qy", None, None),
            P("qx", "qy", None, None),
            P("qx", "qy", None, None),
            P(("qx", "qy"), None, None, None),
            P(),
            P(),
        ),
        out_specs=P(None, "qx", "qy"),
        check_vma=False,
    )
```

profile of v0, /device:TPU:0, one launch (start us, length us, event | category | flops | bytes accessed | tf_op | source)
XLA Modules:
  0.0 75.2 jit_solution(885914404108484808)
XLA Ops:
  0.0 0.7 fusion.6
  0.9 0.7 fusion.5
  1.7 0.6 broadcast_add_fusion.2.refs_0_
  2.3 1.7 %copy.47 = bf16[64,32,128]{0,2,1:T(8,128)(2,1)S(1)} copy(bf16[64,32,128]{2,1,0:T(8,128)(2,1)} %refs_4_.1) | data formatting | bytes 1048576 | tf_op args[0]
  4.1 0.8 %fusion.2.refs_5_ = bf16[2,2,8,16,128]{4,3,2,1,0:T(8,128)(2,1)} fusion(bf16[1,2,16,16,64]{4,3,2,1,0:T(8,128)(2,1)S(1)} %bitcast.61, bf16[1,2,16,16,64]{4,3,2,1,0:T(8,128)(2,1)S(1)} %bitcast.59, bf16[2,2,8,16,64]{4,3,2,1,0:T(8,128)(2,1)S(1)} %fusion.1), kind=kLoop, calls=%fused_computation.16 | loop fusion | flops 393216 | bytes 327680 | tf_op jit(solution)/shard_map/concatenate | solution.py:251
  5.2 0.3 fusion.11
  5.5 1.1 %fusion.12 = f32[8,64,64,1]{2,1,0,3:T(8,128)S(1)} fusion(f32[2,8,64,64]{3,2,1,0:T(8,128)S(1)} %fusion.11, f32[2,8,64,64]{3,2,1,0:T(8,128)S(1)} %copy-done.4), kind=kOutput, calls=%fused_computation.48 | convolution fusion | flops 50331648 | bytes 655360 | tf_op jit(solution)/shard_map/ijrs,ijsv->ijrv/dot_general | solution.py:259
  6.6 0.8 %copy.52.refs_3_ = f32[4,64,64]{2,1,0:T(8,128)} copy(f32[4,64,64]{1,2,0:T(8,128)S(1)} %reduce_sum.48) | data formatting | bytes 131072 | tf_op jit(solution)/shard_map/reduce_sum | solution.py:260
  7.4 20.6 %contrib.1 = (f32[128,32,128]{2,1,0:T(8,128)}, f32[128,128]{1,0:T(8,128)}, bf16[2,64,16,128]{3,2,1,0:T(8,128)(2,1)}, bf16[2,4,8,16,128]{4,3,2,1,0:T(8,128)(2,1)}) custom-call(s32[128]{0:T(128)} %broadcast_add_fusion.2.refs_0_, f32[64,64,128]{2,1,0:T(8,128)} %bitcast.57, f32[16,64,64]{2,1,0:T(8,128)} %bitcast.53, f32[4,64,64]{2,1,0:T(8,128)} %copy.52.refs_3_, ...), custom_call_target="tpu_custom_call" | custom-call | tf_op jit(solution)/shard_map/contrib/pallas_call | solution.py:272
  28.0 0.9 %reduce_max.9 = f32[128]{0:T(128)S(1)} reduce(f32[128,128]{1,0:T(8,128)} %get-tuple-element.13, f32[]{:T(128)} %constant.19.clone.1), dimensions={1}, to_apply=%region_5.6 | reduce | flops 16256 | bytes 66052 | tf_op jit(solution)/shard_map/reduce_max | solution.py:299
  29.1 1.9 %multiply_convert_fusion = f16[128,32,128]{2,1,0:T(8,128)(2,1)S(1)} fusion(f32[128,32,128]{2,1,0:T(8,128)} %get-tuple-element.12, f32[128]{0:T(128)S(1)} %get-tuple-element.29), kind=kLoop, calls=%fused_computation.2 | loop fusion | flops 1048576 | bytes 3146240 | tf_op jit(solution)/shard_map/convert_element_type | solution.py:305
  31.2 1.3 %pad_maximum_fusion.1 = f16[32,132,128]{2,1,0:T(8,128)(2,1)} fusion(f16[32,4,128]{2,1,0:T(4,128)(2,1)S(1)} %broadcast_in_dim.76, f16[32,128,128]{2,1,0:T(8,128)(2,1)S(1)} %bitcast.54), kind=kLoop, calls=%fused_computation.3 | loop fusion | flops 540672 | bytes 2162688 | tf_op jit(solution)/shard_map/concatenate | solution.py:303
  32.5 5.6 %all-to-all-start = ((f16[32,132,128]{2,1,0:T(8,128)(2,1)}), f16[32,132,128]{2,1,0:T(8,128)(2,1)S(1)}, u32[]{:S(2)}, u32[]{:S(2)}) async-start(f16[32,132,128]{2,1,0:T(8,128)(2,1)} %pad_maximum_fusion.1), calls=%async_computation | async-start | bytes 2228224 | tf_op jit(solution)/shard_map/all_to_all | solution.py:311
  38.1 0.3 reduce_window_sum.11
  38.6 1.5 %copy.55 = bf16[2,64,16,128]{1,3,2,0:T(8,128)(2,1)} copy(bf16[2,64,16,128]{3,2,1,0:T(8,128)(2,1)S(1)} %copy-done.3) | data formatting | bytes 1048576 | tf_op jit(solution)/shard_map/optimization_barrier | solution.py:310
  40.0 0.7 copy.59
  40.8 0.6 add.37.refs_0_
  42.1 0.5 copy-done.2
  42.9 3.7 %pad_maximum_fusion.refs_2_ = bf16[64,160,64]{2,1,0:T(8,128)(2,1)} fusion(bf16[64,16,64]{2,1,0:T(8,128)(2,1)S(1)} %bitcast.64, bf16[16,128,64]{2,1,0:T(8,128)(2,1)S(1)} %get-tuple-element.22, bf16[32,128,64]{2,1,0:T(8,128)(2,1)S(1)} %bitcast.51, bf16[16,128,64]{2,1,0:T(8,128)(2,1)S(1)} %get-tuple-element.21, bf16[64,16,64]{2,1,0:T(8,128)(2,1)S(1)} %bitcast.63), kind=kLoop, calls=%fused_computation | loop fusion | flops 6553600 | bytes 2621440 | tf_op jit(solution)/shard_map/concatenate | solution.py:325
  46.6 6.6 %near.1.refs_4_ = f32[16,256,64]{2,1,0:T(8,128)} custom-call(s32[16,3]{1,0:T(8,128)} %bitcast.67, bf16[16,3,256,256]{3,2,1,0:T(8,128)(2,1)} %bitcast.52, bf16[64,160,64]{2,1,0:T(8,128)(2,1)} %pad_maximum_fusion.refs_2_), custom_call_target="tpu_custom_call" | custom-call | flops 402653184 | bytes 6291456 | tf_op jit(solution)/shard_map/near/pallas_call | solution.py:327
  53.2 12.5 %all-to-all-done = f16[32,132,128]{2,1,0:T(8,128)(2,1)S(1)} async-done(((f16[32,132,128]{2,1,0:T(8,128)(2,1)}), f16[32,132,128]{2,1,0:T(8,128)(2,1)S(1)}, u32[]{:S(2)}, u32[]{:S(2)}) %all-to-all-start) | async-done | bytes 1081376 | tf_op jit(solution)/shard_map/all_to_all | solution.py:311
  66.0 0.3 slice.54
  66.3 1.6 %convert_multiply_fusion.refs_1_ = f32[128,32,128]{2,1,0:T(8,128)} fusion(f16[128,32,128]{2,1,0:T(8,128)(2,1)S(1)} %bitcast.55, f32[128]{0:T(128)S(1)} %exp2.46), kind=kLoop, calls=%fused_computation.1 | loop fusion | flops 1048576 | bytes 3146240 | tf_op jit(solution)/shard_map/mul | solution.py:359
  67.9 7.3 %far.1 = f32[64,32,128]{2,1,0:T(8,128)} custom-call(s32[128]{0:T(128)} %add.37.refs_0_, f32[128,32,128]{2,1,0:T(8,128)} %convert_multiply_fusion.refs_1_, f32[16,64,64]{2,1,0:T(8,128)} %bitcast.65, bf16[16,64,256]{2,1,0:T(8,128)(2,1)} %bitcast.66, f32[16,256,64]{2,1,0:T(8,128)} %near.1.refs_4_), custom_call_target="tpu_custom_call" | custom-call | tf_op jit(solution)/shard_map/far/pallas_call | solution.py:360
  (47 shorter events, 2.4 us)
Async XLA Ops:
  0.0 5.2 %copy-start = (bf16[2,8,64,256]{3,2,1,0:T(8,128)(2,1)S(1)}, bf16[2,8,64,256]{3,2,1,0:T(8,128)(2,1)}, u32[]{:S(2)}) copy-start(bf16[2,8,64,256]{3,2,1,0:T(8,128)(2,1)} %param.13) | copy-start | bytes 1572868
  4.1 1.4 %copy-start.4 = (f32[2,8,64,64]{3,2,1,0:T(8,128)S(1)}, f32[2,8,64,64]{3,2,1,0:T(8,128)}, u32[]{:S(2)}) copy-start(f32[2,8,64,64]{3,2,1,0:T(8,128)} %param.15) | copy-start | bytes 786436
  5.5 1.9 %copy-start.1 = (f32[2,8,64,64]{3,2,1,0:T(8,128)}, f32[2,8,64,64]{3,2,1,0:T(8,128)S(1)}, u32[]{:S(2)}) copy-start(f32[2,8,64,64]{3,2,1,0:T(8,128)S(1)} %fusion.11) | copy-start | bytes 786436
  31.0 7.1 %copy-start.6 = (s32[32,128]{1,0:T(8,128)S(1)}, s32[32,128]{1,0:T(8,128)}, u32[]{:S(2)}) copy-start(s32[32,128]{1,0:T(8,128)} %param.18) | copy-start | bytes 49156
  31.0 7.4 %copy-start.7 = (s32[32,128]{1,0:T(8,128)S(1)}, s32[32,128]{1,0:T(8,128)}, u32[]{:S(2)}) copy-start(s32[32,128]{1,0:T(8,128)} %param.19) | copy-start | bytes 49156
  31.0 7.5 %copy-start.3 = (bf16[2,64,16,128]{3,2,1,0:T(8,128)(2,1)S(1)}, bf16[2,64,16,128]{3,2,1,0:T(8,128)(2,1)}, u32[]{:S(2)}) copy-start(bf16[2,64,16,128]{3,2,1,0:T(8,128)(2,1)} %get-tuple-element.18) | copy-start | bytes 1572868
  31.1 8.9 %copy-start.8 = (s32[2,8,3]{1,0,2:T(2,128)S(1)}, s32[2,8,3]{1,0,2:T(2,128)}, u32[]{:S(2)}) copy-start(s32[2,8,3]{1,0,2:T(2,128)} %param.12) | copy-start | bytes 580
  31.2 10.6 %copy-start.5 = (bf16[2,4,8,16,128]{4,3,2,1,0:T(8,128)(2,1)S(1)}, bf16[2,4,8,16,128]{4,3,2,1,0:T(8,128)(2,1)}, u32[]{:S(2)}) copy-start(bf16[2,4,8,16,128]{4,3,2,1,0:T(8,128)(2,1)} %get-tuple-element.17) | copy-start | bytes 786436
  32.5 33.2 %all-to-all-start = ((f16[32,132,128]{2,1,0:T(8,128)(2,1)}), f16[32,132,128]{2,1,0:T(8,128)(2,1)S(1)}, u32[]{:S(2)}, u32[]{:S(2)}) async-start(f16[32,132,128]{2,1,0:T(8,128)(2,1)} %pad_maximum_fusion.1), calls=%async_computation | async-start | bytes 2228224 | tf_op jit(solution)/shard_map/all_to_all | solution.py:311
  41.4 1.2 %copy-start.2 = (bf16[2,64,16,128]{1,3,2,0:T(8,128)(2,1)S(1)}, bf16[2,64,16,128]{1,3,2,0:T(8,128)(2,1)}, u32[]{:S(2)}) copy-start(bf16[2,64,16,128]{1,3,2,0:T(8,128)(2,1)} %copy.55) | copy-start | bytes 1572868
where the time goes:
time: 75.6 us; the launch traced here: 75.2 us
  Pallas kernels  34.5 us (46%)
  other arithmetic  12.9 us (17%)
  waiting for transfers between devices  12.5 us (17%)
  local copies, waits for them, and re-layouts  7.99 us (11%)
  starting transfers between devices  5.55 us (7%)
  matrix products  1.4 us (2%)
    pallas_call x1, Pallas kernels, body(): pl.pallas_call(lambda *refs: first_kernel(leaf_count, upper_count, width_...  20.6 us
    all_to_all x1, waiting for transfers between devices, body(): lax.all_to_all(outgoing, ('qx', 'qy'), split_axis=0, concat_axis=0, tiled...  12.5 us
    pallas_call x1, Pallas kernels, body(): pl.pallas_call(lambda *refs: far_kernel(leaf_x, leaf_y, *refs), out_shape...  7.29 us
    pallas_call x1, Pallas kernels, body(): pl.pallas_call(lambda *refs: near_kernel(leaf_y, *refs), grid=(leaf_count...  6.6 us
    all_to_all x1, starting transfers between devices, body(): lax.all_to_all(outgoing, ('qx', 'qy'), split_axis=0, concat_axis=0, tiled...  5.55 us
    concatenate x1, other arithmetic, body(): grid = jnp.concatenate([near_cols[0], tall, near_cols[1]], axis=1)  3.71 us
    unnamed x20, local copies, waits for them, and re-layouts  2.42 us
    convert_element_type x1, other arithmetic, body(): scaled.reshape(devices, capacity * fold[0], fold[1]).astype(jnp.float16)  1.87 us
  transfers between devices with their start and end apart: 1, of which 1 were waited for; matrix products, arithmetic and copies ran while one was open for 11% of the time, Pallas kernels for 9%

commit v1 on v0

v1 whole, which is shorter than its diff:
```python
import jax
import jax.numpy as jnp
from jax import lax
from jax.experimental import pallas as pl
from jax.experimental.pallas import tpu as pltpu
from jax.sharding import PartitionSpec as P

LS = 16
K0 = 6
K1 = 8
TOP = 15
LANES = 128

ANY = pl.BlockSpec(memory_space=pl.ANY)
VM = pl.BlockSpec(memory_space=pltpu.VMEM)
SM = pl.BlockSpec(memory_space=pltpu.SMEM)
MESH = pl.DeviceIdType.MESH
F32 = jnp.float32
BF16 = jnp.bfloat16
STEPS = [(1, 0), (-1, 0), (0, 1), (0, -1), (1, 1), (1, -1), (-1, 1), (-1, -1)]


def halves(value):
    high = value.astype(BF16)
    return high, (value - high.astype(F32)).astype(BF16)


def product_of(left, right):
    lh, ll = halves(left)
    rh, rl = halves(right)
    return jnp.dot(
        jnp.concatenate([lh, ll, lh, ll], axis=1),
        jnp.concatenate([rh, rh, rl, rl], axis=0),
        preferred_element_type=F32,
    )


def unfolded(value):
    half = value.shape[1] // 2
    return jnp.concatenate([value[:, :half], value[:, half:]], axis=0)


def first_kernel(
    leaf_x,
    leaf_y,
    capacity,
    off_ref,
    dest_any,
    tgt_any,
    vec_any,
    col_any,
    up_any,
    coup_any,
    tiles_any,
    recv_ref,
    rscale_ref,
    near_ref,
    land_ref,
    dest_v,
    tgt_v,
    vec_v,
    col_v,
    up_v,
    coup_v,
    tiles_v,
    vec_f,
    slot_v,
    slot_s,
    coef,
    rhs,
    mats,
    blocks,
    outgo,
    oscale,
    full,
    load_sem,
    tile_sem,
    halo_send,
    halo_recv,
    data_send,
    data_recv,
    scale_send,
    scale_recv,
):
    width_x = lax.axis_size("qx")
    width_y = lax.axis_size("qy")
    devices = width_x * width_y
    here_x = lax.axis_index("qx")
    here_y = lax.axis_index("qy")
    me = here_x * width_y + here_y
    leaf_count = leaf_x * leaf_y
    upper_count = leaf_y // 2
    cluster_count = leaf_count + upper_count
    slot_count = coup_v.shape[2]
    rank = coup_v.shape[0]
    half = rank // 2
    vecs = vec_v.shape[0]
    rows_y = vec_v.shape[2]
    near_count = tiles_v.shape[1]
    pairs = LS // 2
    wide = leaf_y + 2
    i32 = jnp.int32

    loads = [
        pltpu.make_async_copy(src, dst, load_sem.at[n])
        for n, (src, dst) in enumerate(
            (
                (dest_any, dest_v),
                (vec_any, vec_v),
                (col_any, col_v),
                (up_any, up_v),
                (coup_any, coup_v),
                (tgt_any, tgt_v),
            )
        )
    ]
    for load in loads:
        load.start()

    def tile_load(m):
        return pltpu.make_async_copy(tiles_any.at[m], tiles_v.at[m], tile_sem.at[m])

    def peer_of(t):
        u = t // width_y
        turn = lax.rem(u + 1, 2) * -u // 2 + lax.rem(u, 2) * ((u + 1) // 2)
        x = lax.rem(here_x + width_x // 2 + turn + width_x, width_x)
        y = lax.rem(here_y + t + 1, width_y)
        return x, y

    def source_of(t):
        u = t // width_y
        turn = lax.rem(u + 1, 2) * -u // 2 + lax.rem(u, 2) * ((u + 1) // 2)
        x = lax.rem(here_x - width_x // 2 - turn + 2 * width_x, width_x)
        y = lax.rem(here_y - lax.rem(t + 1, width_y) + width_y, width_y)
        return x, y

    barrier = pltpu.get_barrier_semaphore()

    def greet(t, carry):
        pl.semaphore_signal(barrier, inc=1, device_id=peer_of(t), device_id_type=MESH)
        return carry

    lax.fori_loop(0, devices - 1, greet, 0)

    loads[0].wait()
    places = devices * capacity
    own_row = jnp.broadcast_to(dest_v[pl.ds(me, 1), :], (slot_count, slot_count))
    own_col = own_row.T
    ident_row = lax.broadcasted_iota(i32, (slot_count, slot_count), 1)
    ident_col = lax.broadcasted_iota(i32, (slot_count, slot_count), 0)
    before = (own_row == own_col) & (ident_row < ident_col)
    order = jnp.sum(before.astype(F32), axis=1, keepdims=True).astype(i32)
    position = jnp.where(own_col[:, :1] >= 0, own_col[:, :1] * capacity + order, places)
    place = lax.broadcasted_iota(i32, (slot_count, places), 1)
    ident = lax.broadcasted_iota(i32, (slot_count, places), 0)
    chosen = jnp.where(position == place, (ident - slot_count).astype(F32), 0.0)
    slot_v[...] = slot_count + jnp.sum(chosen, axis=0, keepdims=True).astype(i32)

    loads[1].wait()
    vec_f[...] = vec_v[...].astype(F32)

    def block_step(n, carry):
        i = n // pairs
        x = lax.rem(n, pairs)
        first = vec_f[:, i * LS + x, :]
        second = vec_f[:, i * LS + x + pairs, :]
        both = jnp.concatenate([first, second], axis=0).T.astype(BF16)
        for j in range(leaf_y):
            blocks[(i + 1) * wide + j + 1, pl.ds(pl.multiple_of(x * LS, LS), LS), :] = both[j * LS : (j + 1) * LS]
        return carry

    lax.fori_loop(0, leaf_x * pairs, block_step, 0, unroll=2)

    slot_copy = pltpu.make_async_copy(slot_v, slot_s, load_sem.at[len(loads)])
    slot_copy.start()

    def present(dx, dy):
        x = here_x + dx
        y = here_y + dy
        return (x >= 0) & (x < width_x) & (y >= 0) & (y < width_y)

    def halo_spans(dx, dy):
        rows = [1 if dx <= 0 else leaf_x] if dx != 0 else list(range(1, leaf_x + 1))
        land = [0 if dx > 0 else leaf_x + 1] if dx != 0 else rows
        count = leaf_y if dy == 0 else 1
        col = 1 if dy <= 0 else leaf_y
        to = 1 if dy == 0 else (0 if dy > 0 else leaf_y + 1)
        return [(r * wide + col, w * wide + to, count) for r, w in zip(rows, land)]

    def halo_copies(n):
        dx, dy = STEPS[n]
        out = []
        for q, (src, dst, count) in enumerate(halo_spans(dx, dy)):
            out.append(
                pltpu.make_async_remote_copy(
                    src_ref=blocks.at[pl.ds(src, count)],
                    dst_ref=blocks.at[pl.ds(dst, count)],
                    send_sem=halo_send.at[n, q],
                    recv_sem=halo_recv.at[n, q],
                    device_id=(here_x + dx, here_y + dy),
                    device_id_type=MESH,
                )
            )
        return out

    for dx, dy in STEPS:

        @pl.when(jnp.logical_not(present(-dx, -dy)))
        def _():
            for _, dst, count in halo_spans(dx, dy):
                blocks[pl.ds(dst, count)] = jnp.zeros((count,) + blocks.shape[1:], BF16)

    pl.semaphore_wait(barrier, devices - 1)
    for n, (dx, dy) in enumerate(STEPS):

        @pl.when(present(dx, dy))
        def _():
            for copy in halo_copies(n):
                copy.start()

    loads[2].wait()
    diag_zero = jnp.zeros((rank, vecs), BF16)

    def keep(m, value):
        coef[m] = value
        high, low = halves(value)
        top = jnp.concatenate([high, diag_zero, low, diag_zero], axis=1)
        bottom = jnp.concatenate([diag_zero, high, diag_zero, low], axis=1)
        rhs[m] = jnp.concatenate([top, bottom, top, bottom], axis=0)

    def leaf_step(m, carry):
        i = m // leaf_y
        j = lax.rem(m, leaf_y)
        block = unfolded(blocks[(i + 1) * wide + j + 1])
        keep(m, jnp.dot(col_v[m], block, preferred_element_type=F32))
        return carry

    lax.fori_loop(0, leaf_count, leaf_step, 0, unroll=4)
    loads[3].wait()

    def upper_step(p, carry):
        total = None
        for i in range(leaf_x):
            for c in range(2):
                m = i * leaf_y + 2 * p + c
                term = product_of(up_v[m], coef[m])
                total = term if total is None else total + term
        keep(leaf_count + p, total)
        return carry

    lax.fori_loop(0, upper_count, upper_step, 0, unroll=2)

    loads[4].wait()
    for m in range(leaf_count):
        tile_load(m).start()

    def turn_step(r, carry):
        mats[0:slot_count, r, :] = jnp.concatenate([coup_v[r], coup_v[r + half]], axis=0).T
        return carry

    mats[slot_count] = jnp.zeros((half, 2 * rank), F32)
    lax.fori_loop(0, half, turn_step, 0, unroll=2)
    slot_copy.wait()

    def data_copy(t, dst, device):
        return pltpu.make_async_remote_copy(
            src_ref=outgo.at[t],
            dst_ref=recv_ref.at[dst],
            send_sem=data_send.at[t],
            recv_sem=data_recv.at[dst],
            device_id=device,
            device_id_type=MESH,
        )

    def scale_copy(t, dst, device):
        return pltpu.make_async_remote_copy(
            src_ref=oscale.at[t],
            dst_ref=rscale_ref.at[dst],
            send_sem=scale_send.at[t],
            recv_sem=scale_recv.at[dst],
            device_id=device,
            device_id_type=MESH,
        )

    def contribution(p):
        s = jnp.clip(slot_s[0, p], 0, slot_count)
        upper = leaf_count + (s - leaf_count * K0) // K1
        m = jnp.clip(jnp.where(s < leaf_count * K0, s // K0, upper), 0, cluster_count - 1)
        high, low = halves(mats[s])
        res = jnp.dot(jnp.concatenate([high, low], axis=1), rhs[m], preferred_element_type=F32)
        return res[:, : 2 * vecs] + res[:, 2 * vecs :]

    def fill(t):
        x, y = peer_of(t)
        first = (x * width_y + y) * capacity
        values = [contribution(first + k) for k in range(capacity)]
        peak = None
        for value in values:
            size = jnp.abs(value)
            peak = size if peak is None else jnp.maximum(peak, size)
        peak = jnp.max(peak, axis=0, keepdims=True)
        power = jnp.ceil(jnp.log2(jnp.maximum(peak, 1e-30)))
        grow = jnp.exp2(TOP - power)
        oscale[t] = jnp.exp2(power - TOP)
        limit = 2.0**TOP - 1
        for k, value in enumerate(values):
            whole = jnp.clip(jnp.round(value * grow), -limit, limit)
            outgo[t, k * half : (k + 1) * half, :] = whole.astype(i32).astype(jnp.int16)

    def send(t):
        data_copy(t, me, peer_of(t)).start()
        scale_copy(t, me, peer_of(t)).start()

    def dest_step(t, carry):
        fill(t)

        @pl.when(t > 0)
        def _():
            send(t - 1)

        return carry

    lax.fori_loop(0, devices, dest_step, 0, unroll=2)
    own = [
        pltpu.make_async_copy(outgo.at[devices - 1], recv_ref.at[me], data_recv.at[me]),
        pltpu.make_async_copy(oscale.at[devices - 1], rscale_ref.at[me], scale_recv.at[me]),
    ]

    loads[5].wait()
    hits = dest_v[...] == me
    upto = (ident_col < ident_row).astype(BF16)
    ahead = jnp.dot(hits.astype(F32).astype(BF16), upto, preferred_element_type=F32).astype(i32)
    lane = lax.broadcasted_iota(i32, (devices, LANES), 1)
    landing = jnp.zeros((devices, LANES), F32)
    for k in range(capacity):
        taken = jnp.where(hits & (ahead == k), (tgt_v[...] - cluster_count).astype(F32), 0.0)
        landing = jnp.where(lane == k, jnp.sum(taken, axis=1, keepdims=True), landing)
    land_ref[...] = cluster_count + landing.astype(i32)
    for copy in own:
        copy.start()

    for n, (dx, dy) in enumerate(STEPS):

        @pl.when(present(-dx, -dy))
        def _():
            for copy in halo_copies(n):
                copy.wait_recv()

    def near_step(m, carry):
        tile_load(m).wait()
        i = m // leaf_y
        j = lax.rem(m, leaf_y)
        total = None
        for k in range(near_count):
            o = off_ref[m, k]
            block = unfolded(blocks[(i + o // 3) * wide + j + lax.rem(o, 3)])
            term = jnp.dot(tiles_v[m, k], block, preferred_element_type=F32)
            total = term if total is None else total + term
        full[m] = total
        return carry

    lax.fori_loop(0, leaf_count, near_step, 0, unroll=2)
    for i in range(leaf_x):
        for x in range(LS):
            rows = [full[i * leaf_y + j, x * LS : (x + 1) * LS, :] for j in range(leaf_y)]
            near_ref[:, i * LS + x, :] = jnp.concatenate(rows, axis=0).T

    for n, (dx, dy) in enumerate(STEPS):

        @pl.when(present(dx, dy))
        def _():
            for copy in halo_copies(n):
                copy.wait_send()

    def finish(t, carry):
        x, y = source_of(t)
        src = x * width_y + y
        data_copy(t, src, (x, y)).wait_recv()
        scale_copy(t, src, (x, y)).wait_recv()
        data_copy(t, me, peer_of(t)).wait_send()
        scale_copy(t, me, peer_of(t)).wait_send()
        return carry

    lax.fori_loop(0, devices - 1, finish, 0)
    for copy in own:
        copy.wait()


def far_kernel(leaf_x, leaf_y, capacity, land_ref, recv_ref, rscale_ref, down_ref, row_ref, near_ref, out_ref, acc, full):
    leaf_count = leaf_x * leaf_y
    half = acc.shape[1]
    acc[...] = jnp.zeros_like(acc)

    def add(src, carry):
        scale = rscale_ref[src]
        for k in range(capacity):
            t = land_ref[src, k]
            acc[t] = acc[t] + recv_ref[src, k * half : (k + 1) * half, :].astype(F32) * scale
        return carry

    lax.fori_loop(0, recv_ref.shape[0], add, 0, unroll=2)

    def leaf(m, carry):
        j = lax.rem(m, leaf_y)
        value = unfolded(acc[m]) + product_of(down_ref[m], unfolded(acc[leaf_count + j // 2]))
        high, low = halves(value)
        basis = row_ref[m]
        full[m] = lax.dot_general(
            jnp.concatenate([basis, basis], axis=0),
            jnp.concatenate([high, low], axis=0),
            (((0,), (0,)), ((), ())),
            preferred_element_type=F32,
        )
        return carry

    lax.fori_loop(0, leaf_count, leaf, 0, unroll=4)
    for a in range(leaf_x):
        for i in range(LS):
            rows = [full[a * leaf_y + h, i * LS : (i + 1) * LS, :] for h in range(leaf_y)]
            x = a * LS + i
            out_ref[:, x, :] = near_ref[:, x, :] + jnp.concatenate(rows, axis=0).T


def body(
    vectors,
    near_tiles,
    near_offset,
    col_basis,
    row_basis,
    up_transfer,
    down_transfer,
    coupling,
    couple_dest,
    couple_target,
):
    shape = jax.ShapeDtypeStruct
    devices = lax.axis_size("qx") * lax.axis_size("qy")
    vec_count, rows_x, rows_y = vectors.shape
    leaf_x = rows_x // LS
    leaf_y = rows_y // LS
    leaf_count = leaf_x * leaf_y
    cluster_count = leaf_count + leaf_y // 2
    rank = coupling.shape[2]
    slot_count = coupling.shape[1]
    capacity = (slot_count + devices - 1) // devices
    near_count = near_tiles.shape[2]
    points = LS * LS
    half = rank // 2
    block = (points // 2, 2 * vec_count)
    dma = pltpu.SemaphoreType.DMA

    recv, rscale, near, land = pl.pallas_call(
        lambda *refs: first_kernel(leaf_x, leaf_y, capacity, *refs),
        out_shape=(
            shape((devices, capacity * half, 2 * vec_count), jnp.int16),
            shape((devices, 1, 2 * vec_count), F32),
            shape((vec_count, rows_x, rows_y), F32),
            shape((devices, LANES), jnp.int32),
        ),
        in_specs=[SM] + [ANY] * 7,
        out_specs=(ANY, ANY, VM, VM),
        scratch_shapes=[
            pltpu.VMEM(couple_dest.shape, jnp.int32),
            pltpu.VMEM(couple_target.shape, jnp.int32),
            pltpu.VMEM(vectors.shape, BF16),
            pltpu.VMEM((leaf_count, rank, points), BF16),
            pltpu.VMEM((leaf_count, rank, rank), F32),
            pltpu.VMEM((rank, rank, slot_count), F32),
            pltpu.VMEM((leaf_count, near_count, points, points), BF16),
            pltpu.VMEM(vectors.shape, F32),
            pltpu.VMEM((1, devices * capacity), jnp.int32),
            pltpu.SMEM((1, devices * capacity), jnp.int32),
            pltpu.VMEM((cluster_count, rank, vec_count), F32),
            pltpu.VMEM((cluster_count, 4 * rank, 4 * vec_count), BF16),
            pltpu.VMEM((slot_count + 1, half, 2 * rank), F32),
            pltpu.VMEM(((leaf_x + 2) * (leaf_y + 2),) + block, BF16),
            pltpu.VMEM((devices, capacity * half, 2 * vec_count), jnp.int16),
            pltpu.VMEM((devices, 1, 2 * vec_count), F32),
            pltpu.VMEM((leaf_count, points, vec_count), F32),
            dma((7,)),
            dma((leaf_count,)),
            dma((len(STEPS), leaf_x)),
            dma((len(STEPS), leaf_x)),
            dma((devices,)),
            dma((devices,)),
            dma((devices,)),
            dma((devices,)),
        ],
        compiler_params=pltpu.CompilerParams(collective_id=0, has_side_effects=True),
        name="send",
    )(
        near_offset.reshape(leaf_count, near_count),
        couple_dest,
        couple_target,
        vectors,
        col_basis.reshape(leaf_count, rank, points),
        up_transfer.reshape(leaf_count, rank, rank),
        coupling[0].transpose(1, 2, 0),
        near_tiles.reshape(leaf_count, near_count, points, points),
    )

    return pl.pallas_call(
        lambda *refs: far_kernel(leaf_x, leaf_y, capacity, *refs),
        out_shape=shape((vec_count, rows_x, rows_y), F32),
        in_specs=[SM, VM, VM, VM, VM, VM],
        out_specs=VM,
        scratch_shapes=[
            pltpu.VMEM((cluster_count + 1, half, 2 * vec_count), F32),
            pltpu.VMEM((leaf_count, points, vec_count), F32),
        ],
        name="far",
    )(
        land,
        recv,
        rscale,
        down_transfer.reshape(leaf_count, rank, rank),
        row_basis.reshape(leaf_count, rank, points),
        near,
    )


def solution(mesh):
    return jax.shard_map(
        body,
        mesh=mesh,
        in_specs=(
            P(None, "qx", "qy"),
            P("qx", "qy", None, None, None),
            P("qx", "qy", None),
            P("qx", "qy", None, None),
            P("qx", "qy", None, None),
            P("qx", "qy", None, None),
            P("qx", "qy", None, None),
            P(("qx", "qy"), None, None, None),
            P(),
            P(),
        ),
        out_specs=P(None, "qx", "qy"),
        check_vma=False,
    )
```

time: 75.6 us -> 49.3 us (0.65)
  the two profiles are of different devices: /device:TPU:0 before, /device:TPU:12 now
where the time goes in v1:
time: 49.3 us; the launch traced here: 49 us
  Pallas kernels  47.6 us (97%)
  local copies, waits for them, and re-layouts  1.36 us (3%)
    pallas_call x1, Pallas kernels, body(): pl.pallas_call(lambda *refs: first_kernel(leaf_x, leaf_y, capacity, *refs...  40.6 us
    pallas_call x1, Pallas kernels, body(): pl.pallas_call(lambda *refs: far_kernel(leaf_x, leaf_y, capacity, *refs),...  7.08 us
    reshape x1, local copies, waits for them, and re-layouts, body(): near_offset.reshape(leaf_count, near_count)  1.36 us

profile of v1, /device:TPU:12, one launch (start us, length us, event | category | flops | bytes accessed | tf_op | source)
XLA Modules:
  0.0 49.0 jit_solution(14776326346697066642)
XLA Ops:
  0.0 1.4 %copy.12 = s32[2,8,3]{2,1,0:T(8,128)} copy(s32[2,8,3]{1,0,2:T(2,128)} %param.12) | data formatting | bytes 384 | tf_op jit(solution)/shard_map/reshape | solution.py:492
  1.4 40.6 %send.1 = (s16[32,128,128]{2,1,0:T(8,128)(2,1)}, f32[32,1,128]{2,1,0:T(1,128)}, f32[64,32,128]{2,1,0:T(8,128)}, s32[32,128]{1,0:T(8,128)}) custom-call(s32[16,3]{1,0:T(8,128)} %bitcast.15, s32[32,128]{1,0:T(8,128)} %refs_1_.1, s32[32,128]{1,0:T(8,128)} %refs_2_.1, bf16[64,32,128]{2,1,0:T(8,128)(2,1)} %refs_3_.1, bf16[16,64,256]{2,1,0:T(8,128)(2,1)} %bitcast.11, ...), custom_call_target="tpu_custom_call" | custom-call | tf_op jit(solution)/shard_map/send/pallas_call | solution.py:452
  41.9 7.1 %far.1 = f32[64,32,128]{2,1,0:T(8,128)} custom-call(s32[32,128]{1,0:T(8,128)} %get-tuple-element.9.refs_0_, s16[32,128,128]{2,1,0:T(8,128)(2,1)} %get-tuple-element.10.refs_1_, f32[32,1,128]{2,1,0:T(1,128)} %get-tuple-element.11.refs_2_, f32[16,64,64]{2,1,0:T(8,128)} %bitcast.13, bf16[16,64,256]{2,1,0:T(8,128)(2,1)} %bitcast.14, ...), custom_call_target="tpu_custom_call" | custom-call | tf_op jit(solution)/shard_map/far/pallas_call | solution.py:502
